TPU v7x, 32 devices: a whole 2x2x4 slice. The times are simulated.
32 devices in a mesh: row: 8 (over z, y), col: 4 (over x, core).
Axes of the slice: x: 2, y: 2, z: 4, core: 2. Of those that a mesh axis runs over, the one named last changes fastest.
Arguments:
- entries: int32 [32, 16, 128, 128], P('row', 'col'), may hold values from -2 to 2
- tile_cols: int32 [32, 16], P('row', 'col'), may hold values from 0 to 31
- block_now: int32 [32, 16384], P(None, ('col', 'row')), may hold values from 0 to 65520
- block_prev: int32 [32, 16384], P(None, ('col', 'row')), may hold values from 0 to 65520
- block_prev2: int32 [32, 16384], P(None, ('col', 'row')), may hold values from 0 to 65520
- gram_prev: int32 [32, 32], replicated, may hold values from 0 to 65520
- square_prev: int32 [32, 32], replicated, may hold values from 0 to 65520
- inverse_prev: int32 [32, 32], replicated, may hold values from 0 to 65520
- inverse_prev2: int32 [32, 32], replicated, may hold values from 0 to 65520
Outputs:
- next_block: float32 [32, 16384], P(None, ('col', 'row'))
- later_block: float32 [32, 16384], P(None, ('col', 'row'))
Inputs may be any that keep to these rules, and one draw needn't show every extreme that they name: `tile_cols`: stored tiles that name the same tile column in one tile row add. `block_prev`: residues. `block_prev2`: residues. `gram_prev`: residues. `square_prev`: residues. `inverse_prev`: residues. `inverse_prev2`: residues.
All inputs are finite; a program needn't handle non-finite values.
Results may differ from a plain program's by a relative error of at most 0.0003.
Values sent between devices are 32-bit elements; how exact they have to be, the bound alone decides.
A program may use at most 64 MiB of HBM per device.

v0:
```python
import jax
import jax.numpy as jnp
from jax import lax
from jax.sharding import PartitionSpec as P

modulus = 65521.0


def residue(values):
    return jnp.mod(values, modulus)


def split_digits(values):
    top_part = jnp.floor(values / 256.0)
    return (top_part, values - top_part * 256.0)


def fold_digits(top_sum, low_sum):
    return residue(residue(residue(top_sum) * 256.0) + residue(low_sum))


def fold_three(upper_part, middle, lower_part):
    return residue(
        residue(residue(upper_part) * 15.0) + residue(residue(middle) * 256.0) + residue(lower_part)
    )


def mulmod(left_side, right_side):
    top_part, low_part = split_digits(right_side)
    return fold_digits(left_side * top_part, left_side * low_part)


def exact_dot(left_side, right_side):
    return jnp.dot(
        left_side, right_side, precision=lax.Precision.HIGHEST, preferred_element_type=jnp.float32
    )


def small_product(left_side, right_side):
    left_top, left_low = split_digits(left_side)
    right_top, right_low = split_digits(right_side)
    return fold_three(
        exact_dot(left_top, right_top),
        exact_dot(left_top, right_low) + exact_dot(left_low, right_top),
        exact_dot(left_low, right_low),
    )


def inverse_scalar(number):
    result = jnp.ones_like(number)
    square = number
    exponent = 65519
    for position in range(16):
        if exponent >> position & 1:
            result = mulmod(result, square)
        square = mulmod(square, square)
    return result


def inverse_matrix(matrix):
    matrix_order = matrix.shape[0]
    augmented = jnp.concatenate([matrix, jnp.eye(matrix_order, dtype=matrix.dtype)], axis=1)
    row_numbers = jnp.arange(matrix_order, dtype=jnp.int32)

    def eliminate(column, augmented):
        column = jnp.asarray(column).astype(jnp.int32)
        pivot_column = augmented[:, column]
        usable = (pivot_column != 0.0) & (row_numbers >= column)
        pivot_row_id = jnp.where(jnp.any(usable), jnp.argmax(usable), column)
        pivot_row = augmented[pivot_row_id]
        current_row = augmented[column]
        swapped = jnp.where(
            (row_numbers == column)[:, None],
            pivot_row[None, :],
            jnp.where((row_numbers == pivot_row_id)[:, None], current_row[None, :], augmented),
        )
        scaled = mulmod(pivot_row, inverse_scalar(pivot_row[column]))
        factors = jnp.where(row_numbers == column, 0.0, swapped[:, column])
        reduced = residue(swapped - mulmod(factors[:, None], scaled[None, :]) + modulus)
        return jnp.where((row_numbers == column)[:, None], scaled[None, :], reduced)

    augmented = lax.fori_loop(0, matrix_order, eliminate, augmented)
    return augmented[:, matrix_order:]


def coefficients(
    gram_now, square_now, inverse_now, inverse_prev, inverse_prev2, gram_old, square_old
):
    identity = jnp.eye(gram_now.shape[0], dtype=gram_now.dtype)
    first = residue(identity - small_product(residue(square_now + gram_now), inverse_now) + modulus)
    second = residue(modulus - small_product(gram_now, inverse_prev))
    middle = residue(identity - small_product(inverse_prev, gram_old) + modulus)
    third = residue(
        modulus
        - small_product(small_product(residue(square_old + gram_old), middle), inverse_prev2)
    )
    return jnp.concatenate([first, second, third], axis=1)


def digit_stack(values):
    top_part, low_part = split_digits(values)
    return jnp.stack([top_part, low_part]).astype(jnp.bfloat16)


def combine_blocks(coeffs, stacked):
    products = jnp.einsum(
        "dab,ebn->dean",
        digit_stack(coeffs),
        digit_stack(stacked),
        preferred_element_type=jnp.float32,
    )
    return fold_three(products[0, 0], products[0, 1] + products[1, 0], products[1, 1])


def gram_local(first, second):
    column_count = first.shape[1]
    group_width = min(column_count, 128)
    groups = column_count // group_width
    first_digits = digit_stack(first).reshape(2, first.shape[0], groups, group_width)
    second_digits = digit_stack(second).reshape(2, second.shape[0], groups, group_width)
    products = jnp.einsum(
        "dagw,ecgw->gdeac", first_digits, second_digits, preferred_element_type=jnp.float32
    )
    per_group = fold_three(
        products[:, 0, 0], products[:, 0, 1] + products[:, 1, 0], products[:, 1, 1]
    )
    return residue(jnp.sum(per_group, axis=0))


def digit_pair(values):
    top_part, low_part = split_digits(values)
    return jnp.stack([top_part, low_part])


def forward_partial(block_full, tile_values, tile_cols):
    tile_rows, slot_count, tile_size = (
        tile_values.shape[0],
        tile_values.shape[1],
        tile_values.shape[2],
    )
    block_rows = block_full.shape[0]
    top_part, low_part = split_digits(block_full)
    digits = jnp.concatenate([top_part, low_part], axis=0).astype(jnp.bfloat16)
    digits = digits.reshape(2 * block_rows, -1, tile_size)
    picked = jnp.take(digits, tile_cols.reshape(-1), axis=1).reshape(
        2 * block_rows, tile_rows, slot_count, tile_size
    )
    raw_sums = jnp.einsum("brsk,rsjk->brj", picked, tile_values, preferred_element_type=jnp.float32)
    return fold_digits(raw_sums[:block_rows], raw_sums[block_rows:]).reshape(
        block_rows, tile_rows * tile_size
    )


def backward_partial(projected, tile_values, onehot):
    tile_rows, tile_size = (tile_values.shape[0], tile_values.shape[2])
    block_rows = projected.shape[0]
    top_part, low_part = split_digits(projected)
    digits = (
        jnp.concatenate([top_part, low_part], axis=0)
        .astype(jnp.bfloat16)
        .reshape(2 * block_rows, tile_rows, tile_size)
    )
    spread = jnp.einsum("brj,rsjk->brsk", digits, tile_values, preferred_element_type=jnp.float32)
    raw_sums = jnp.einsum(
        "brsk,rsc->bck",
        spread,
        onehot,
        precision=lax.Precision.HIGHEST,
        preferred_element_type=jnp.float32,
    )
    return fold_digits(raw_sums[:block_rows], raw_sums[block_rows:]).reshape(block_rows, -1)


def body(
    entries,
    tile_cols,
    block_now,
    block_prev,
    block_prev2,
    gram_prev,
    square_prev,
    inverse_prev,
    inverse_prev2,
):
    tile_values = entries.astype(jnp.bfloat16)
    tile_size = tile_values.shape[2]
    share_width = block_now.shape[1]
    col_tiles = share_width * lax.axis_size("row") // tile_size
    onehot = (
        tile_cols[:, :, None] == jnp.arange(col_tiles, dtype=jnp.int32)[None, None, :]
    ).astype(jnp.float32)
    current = block_now.astype(jnp.float32)
    earlier = block_prev.astype(jnp.float32)
    earliest = block_prev2.astype(jnp.float32)
    gram_old = gram_prev.astype(jnp.float32)
    square_old = square_prev.astype(jnp.float32)
    inverse_old = inverse_prev.astype(jnp.float32)
    inverse_older = inverse_prev2.astype(jnp.float32)
    results = []
    for iteration in range(2):
        block_full = lax.all_gather(current, "row", axis=1, tiled=True)
        projected = residue(lax.psum(forward_partial(block_full, tile_values, tile_cols), "col"))
        piece_width = projected.shape[1] // lax.axis_size("col")
        projected_piece = lax.dynamic_slice_in_dim(
            projected, lax.axis_index("col") * piece_width, piece_width, 1
        )
        gram_digits = lax.psum(
            digit_pair(gram_local(projected_piece, projected_piece)), ("row", "col")
        )
        partial_term = backward_partial(projected, tile_values, onehot)
        applied = residue(lax.psum_scatter(partial_term, "row", scatter_dimension=1, tiled=True))
        square_digits = lax.psum(digit_pair(gram_local(applied, applied)), ("row", "col"))
        gram_now = fold_digits(gram_digits[0], gram_digits[1])
        square_now = fold_digits(square_digits[0], square_digits[1])
        inverse_now = inverse_matrix(gram_now)
        coeffs = coefficients(
            gram_now, square_now, inverse_now, inverse_old, inverse_older, gram_old, square_old
        )
        stacked = jnp.concatenate([current, earlier, earliest], axis=0)
        following = residue(applied + combine_blocks(coeffs, stacked))
        results.append(following / modulus)
        earliest, earlier, current = (earlier, current, following)
        inverse_older, inverse_old = (inverse_old, inverse_now)
        gram_old, square_old = (gram_now, square_now)
    return (results[0], results[1])


def solution(mesh):
    placed = (
        P("row", "col", None, None),
        P("row", "col"),
        P(None, ("col", "row")),
        P(None, ("col", "row")),
        P(None, ("col", "row")),
        P(),
        P(),
        P(),
        P(),
    )
    return jax.shard_map(
        body,
        mesh=mesh,
        in_specs=placed,
        out_specs=(P(None, ("col", "row")), P(None, ("col", "row"))),
        check_vma=False,
    )
```

profile of v0, /device:TPU:0, one launch (start us, length us, event | category | flops | bytes accessed | tf_op | source)
XLA Modules:
  0.0 1182.8 jit_solution(15742757595589438202)
XLA Ops:
  7.2 0.8 reshape.1208
  8.1 0.9 fusion.475
  8.9 33.0 %all_gather.6 = f32[32,4096]{1,0:T(8,128)S(1)} all-gather(f32[32,512]{1,0:T(8,128)S(1)} %get-tuple-element.317), channel_id=1, replica_groups=mesh['row'=8,'col'=4] {'row'}, dimensions={1}, use_global_device_ids=true | all-gather | bytes 589824 | tf_op jit(solution)/shard_map/all_gather | solution.py:201
  43.4 0.8 copy_bitcast_fusion.7
  48.3 28.7 %all-reduce.5.cloned.1.call-done = f32[32,512]{1,0:T(8,128)} async-done(((f32[32,512]{1,0:T(8,128)}), f32[32,512]{1,0:T(8,128)}) %all-reduce.5.cloned.1.call-update) | async-done | bytes 65552 | tf_op jit(solution)/shard_map/psum | solution.py:202
  77.0 0.9 fusion.161
  78.6 1.1 convolution_bitcast_fusion.1
  79.7 1.1 add_select_fusion.22
  80.8 1.1 copy.394
  83.2 62.1 %reduce-scatter.3.cloned.1.call-done = f32[32,512]{1,0:T(8,128)} async-done(((f32[32,4096]{1,0:T(8,128)}), f32[32,512]{1,0:T(8,128)}) %reduce-scatter.3.cloned.1.call-update) | async-done | bytes 65552 | tf_op jit(solution)/shard_map/reduce_scatter | solution.py:211
  145.3 0.9 subtract_convert_fusion.6
  146.7 40.5 %all-reduce.1 = (f32[2,32,32]{1,2,0:T(8,128)S(1)}, f32[2,32,32]{1,2,0:T(8,128)S(1)}) all-reduce(f32[2,32,32]{1,2,0:T(8,128)S(1)} %pad_maximum_fusion.7, f32[2,32,32]{1,2,0:T(8,128)S(1)} %pad_maximum_fusion.6), channel_id=1, replica_groups=mesh['row'=8,'col'=4] {'row','col'}, use_global_device_ids=true, to_apply=%region_4.6 | all-reduce | flops 4096 | bytes 32768 | tf_op jit(solution)/shard_map/psum | solution.py:207
  187.4 403.5 %while.36 = (s32[]{:T(128)}, f32[32,64]{0,1:T(8,128)S(1)}, s32[]{:T(128)}, s32[]{:T(128)}, s32[]{:T(128)}, /*index=5*/s32[]{:T(128)}, s32[]{:T(128)}, f32[]{:T(128)}, f32[]{:T(128)}, f32[]{:T(128)}, /*index=10*/f32[]{:T(128)}) while((s32[]{:T(128)}, f32[32,64]{0,1:T(8,128)S(1)}, s32[]{:T(128)}, s32[]{:T(128)}, ...), condition=%wide.region_8.10_spmd.clone.clone, body=%wide.region_5.9_spmd.clone.clone.sunk | while | flops 87498 | bytes 50118 | solution.py:82
  188.0 0.7 iota_reduce_fusion.4
  200.6 0.7 iota_reduce_fusion.4
  213.2 0.7 iota_reduce_fusion.4
  225.9 0.7 iota_reduce_fusion.4
  238.5 0.7 iota_reduce_fusion.4
  377.2 0.7 iota_reduce_fusion.4
  389.8 0.7 iota_reduce_fusion.4
  402.4 0.7 iota_reduce_fusion.4
  415.0 0.7 iota_reduce_fusion.4
  427.6 0.7 iota_reduce_fusion.4
  440.2 0.7 iota_reduce_fusion.4
  452.8 0.7 iota_reduce_fusion.4
  465.4 0.7 iota_reduce_fusion.4
  478.0 0.7 iota_reduce_fusion.4
  594.2 0.9 broadcast_multiply_fusion
  595.2 31.4 %all_gather.7 = f32[32,4096]{1,0:T(8,128)S(1)} all-gather(f32[32,512]{1,0:T(8,128)S(1)} %get-tuple-element.284), channel_id=1, replica_groups=mesh['row'=8,'col'=4] {'row'}, dimensions={1}, use_global_device_ids=true | all-gather | bytes 589824 | tf_op jit(solution)/shard_map/all_gather | solution.py:201
  627.8 0.8 copy_bitcast_fusion.6
  629.5 30.0 %all-reduce.7.cloned.1.call-done = f32[32,512]{1,0:T(8,128)} async-done(((f32[32,512]{1,0:T(8,128)}), f32[32,512]{1,0:T(8,128)}) %all-reduce.7.cloned.1.call-update) | async-done | bytes 65552 | tf_op jit(solution)/shard_map/psum | solution.py:202
  659.5 0.9 fusion.163
  660.7 1.1 convolution_bitcast_fusion
  661.7 1.1 add_select_fusion.18
  662.9 1.1 copy.393
  664.8 62.5 %reduce-scatter.5.cloned.1.call-done = f32[32,512]{1,0:T(8,128)} async-done(((f32[32,4096]{1,0:T(8,128)}), f32[32,512]{1,0:T(8,128)}) %reduce-scatter.5.cloned.1.call-update) | async-done | bytes 65552 | tf_op jit(solution)/shard_map/reduce_scatter | solution.py:211
  727.3 0.9 fusion.157
  728.8 40.6 %all-reduce = (f32[2,32,32]{1,2,0:T(8,128)S(1)}, f32[2,32,32]{1,2,0:T(8,128)S(1)}) all-reduce(f32[2,32,32]{1,2,0:T(8,128)S(1)} %pad_maximum_fusion.9, f32[2,32,32]{1,2,0:T(8,128)S(1)} %pad_maximum_fusion.8), channel_id=1, replica_groups=mesh['row'=8,'col'=4] {'row','col'}, use_global_device_ids=true, to_apply=%region_13.15 | all-reduce | flops 4096 | bytes 32768 | tf_op jit(solution)/shard_map/psum | solution.py:207
  769.5 403.5 %while.37 = (s32[]{:T(128)}, f32[32,64]{0,1:T(8,128)S(1)}, s32[]{:T(128)}, s32[]{:T(128)}, s32[]{:T(128)}, /*index=5*/s32[]{:T(128)}, s32[]{:T(128)}, f32[]{:T(128)}, f32[]{:T(128)}, f32[]{:T(128)}, /*index=10*/f32[]{:T(128)}) while((s32[]{:T(128)}, f32[32,64]{0,1:T(8,128)S(1)}, s32[]{:T(128)}, s32[]{:T(128)}, ...), condition=%wide.region_17.19_spmd.clone.clone, body=%wide.region_14.18_spmd.clone.clone.sunk | while | flops 87498 | bytes 50118 | solution.py:82
  770.1 0.7 iota_reduce_fusion.5
  782.7 0.7 iota_reduce_fusion.5
  795.3 0.7 iota_reduce_fusion.5
  808.0 0.7 iota_reduce_fusion.5
  820.6 0.7 iota_reduce_fusion.5
  833.2 0.7 iota_reduce_fusion.5
  845.8 0.7 iota_reduce_fusion.5
  858.4 0.7 iota_reduce_fusion.5
  1175.4 0.9 fusion.130
  (694 shorter events, 167.6 us)
Async XLA Ops:
  7.2 34.9 %copy-start = (s32[4,4,128,128]{3,2,1,0:T(8,128)S(1)}, s32[4,4,128,128]{3,2,1,0:T(8,128)}, u32[]{:S(2)}) copy-start(s32[4,4,128,128]{3,2,1,0:T(8,128)} %param.15) | copy-start | bytes 3145732
  7.2 69.8 %all-reduce.5.cloned.1.call-start = ((), (), s32[]{:S(2)}) async-start(), calls=%async_computation.2 | async-start | bytes 131072 | tf_op jit(solution)/shard_map/psum | solution.py:202
  44.2 0.7 copy-start.6
  44.2 0.8 copy-start.7
  44.2 101.1 %reduce-scatter.3.cloned.1.call-start = ((), (), s32[]{:S(2)}) async-start(), calls=%async_computation.3 | async-start | bytes 589824 | tf_op jit(solution)/shard_map/reduce_scatter | solution.py:211
  45.3 0.7 copy-start.8
  46.7 0.7 copy-start.9
  77.9 0.7 copy-start.5
  81.9 0.8 copy-start.4
  81.9 0.9 copy-start.3
  82.0 577.6 %all-reduce.7.cloned.1.call-start = ((), (), s32[]{:S(2)}) async-start(), calls=%async_computation.4 | async-start | bytes 131072 | tf_op jit(solution)/shard_map/psum | solution.py:202
  593.4 0.8 copy-start.1
  628.6 98.7 %reduce-scatter.5.cloned.1.call-start = ((), (), s32[]{:S(2)}) async-start(), calls=%async_computation.5 | async-start | bytes 589824 | tf_op jit(solution)/shard_map/reduce_scatter | solution.py:211
  1174.5 0.8 copy-start.2
Sparse Core Ops, SparseCore 0:
  44.3 32.6 all-reduce.4
  82.1 63.1 reduce-scatter.2
  628.7 30.7 all-reduce.6
  664.1 63.1 reduce-scatter.4
where the time goes:
time: 1190 us; the launch traced here: 1180 us
  loops' own time  641 us (54%)
  waiting for transfers between devices  183 us (15%)
  blocking collectives  146 us (12%)
  other arithmetic  141 us (12%)
  local copies, waits for them, and re-layouts  47.1 us (4%)
  between operations  14.5 us (1%)
    another operation x2, loops' own time, inverse_matrix(): augmented = lax.fori_loop(0, matrix_order, eliminate, augmented)  641 us
    reduce_scatter x2, waiting for transfers between devices, body(): lax.psum_scatter(partial_term, 'row', scatter_dimension=1, tiled=True)  125 us
    psum x2, blocking collectives, body(): lax.psum(digit_pair(gram_local(projected_piece, projected_piece)), ('row'...  81.1 us
    all_gather x2, blocking collectives, body(): block_full = lax.all_gather(current, 'row', axis=1, tiled=True)  64.4 us
    psum x2, waiting for transfers between devices, body(): lax.psum(forward_partial(block_full, tile_values, tile_cols), 'col')  58.7 us
    another operation x64, other arithmetic, eliminate(): pivot_row_id = jnp.where(jnp.any(usable), jnp.argmax(usable), column)  46.5 us
    eq x64, other arithmetic, eliminate(): return jnp.where((row_numbers == column)[:, None], scaled[None, :], reduced)  41.2 us
    dynamic_slice x64, local copies, waits for them, and re-layouts, eliminate(): scaled = mulmod(pivot_row, inverse_scalar(pivot_row[column]))  37.6 us
  transfers between devices with their start and end apart: 4, of which 4 were waited for; matrix products, arithmetic and copies ran while one was open for 0% of the time, Pallas kernels for 0%

commit v1 on v0

v1 whole, which is shorter than its diff:
```python
import functools

import jax
import jax.numpy as jnp
from jax import lax
from jax.experimental import pallas as pl
from jax.experimental.pallas import tpu as pltpu
from jax.sharding import PartitionSpec as P

modulus = 65521.0
reciprocal = 1.0 / 65521.0
MESH = pl.DeviceIdType.MESH
GATHER, PARTIAL, SCATTER, GRAM, SQUARE_ROW, SQUARE_COL = range(6)


def near(values):
    return values - jnp.floor(values * reciprocal + 0.5) * modulus


def whole(values):
    signed = near(values)
    return jnp.where(signed < 0.0, signed + modulus, signed)


def split(values):
    top = jnp.floor(values * (1.0 / 256.0) + 0.5)
    return top, values - top * 256.0


def digits(values):
    top, low = split(values)
    return jnp.concatenate([top, low], axis=0).astype(jnp.bfloat16)


def fold_two(top, low):
    return near(near(top) * 256.0 + low)


def fold_three(upper, middle, lower):
    return near(near(upper) * 15.0 + near(middle) * 256.0 + near(lower))


def mulmod(left, right):
    top, low = split(right)
    return near(near(left * top) * 256.0 + left * low)


def dot(left, right):
    return jnp.dot(left, right, preferred_element_type=jnp.float32)


def dot_t(left, right):
    return lax.dot_general(
        left, right, (((1,), (1,)), ((), ())), preferred_element_type=jnp.float32
    )


def product_parts(left, right):
    order = left.shape[0]
    left_digits = digits(left)
    right_top, right_low = split(right)
    with_top = dot(left_digits, right_top.astype(jnp.bfloat16))
    with_low = dot(left_digits, right_low.astype(jnp.bfloat16))
    return with_top[:order], with_top[order:] + with_low[:order], with_low[order:]


def small_product(left, right):
    return fold_three(*product_parts(left, right))


def gram_tiles(tiles):
    order = tiles[0].shape[0]
    total = None
    for tile in tiles:
        both = digits(tile)
        term = dot_t(both, both)
        total = term if total is None else total + term
    return fold_three(
        total[:order, :order],
        total[:order, order:] + total[order:, :order],
        total[order:, order:],
    )


def power_inverse(number):
    result = None
    square = number
    for position in range(16):
        if 65519 >> position & 1:
            result = square if result is None else mulmod(result, square)
        if position < 15:
            square = mulmod(square, square)
    return result


def identity_of(order):
    rows = lax.broadcasted_iota(jnp.int32, (order, order), 0)
    lanes = lax.broadcasted_iota(jnp.int32, (order, order), 1)
    return jnp.where(rows == lanes, 1.0, 0.0).astype(jnp.float32)


def inverse_of(matrix):
    order = matrix.shape[0]
    work = jnp.concatenate([matrix, identity_of(order)], axis=1)
    rows = lax.broadcasted_iota(jnp.int32, (order, 1), 0)
    for column in range(order):
        entry = work[:, column : column + 1]
        usable = (entry != 0.0) & (rows >= column)
        first = jnp.min(jnp.where(usable, rows, order), axis=0, keepdims=True)
        chosen = rows == jnp.where(first == order, column, first)
        pivot_row = jnp.sum(jnp.where(chosen, work, 0.0), axis=0, keepdims=True)
        pivot = jnp.sum(jnp.where(chosen, entry, 0.0), axis=0, keepdims=True)
        swapped = jnp.where(chosen, work[column : column + 1, :], work)
        factor = jnp.where(chosen, entry[column : column + 1, :], entry)
        pivot_row = jnp.where(pivot == 0.0, 0.0, pivot_row)
        pivot = jnp.where(pivot == 0.0, 1.0, pivot)
        pivot_top, pivot_low = split(pivot)
        factor_top, factor_low = split(factor)
        upper = near(pivot_top * swapped - factor_top * pivot_row)
        reduced = near(upper * 256.0 + (pivot_low * swapped - factor_low * pivot_row))
        work = jnp.where(rows == column, pivot_row, reduced)
    left = work[:, :order]
    diagonal = jnp.sum(left * identity_of(order), axis=1, keepdims=True)
    return mulmod(work[:, order:], power_inverse(diagonal))


def kernel(
    n_row, n_col, index_ref, entries_ref, now_ref, prev_ref, prev2_ref,
    gram_ref, square_ref, inverse_ref, inverse2_ref, next_ref, later_ref,
    tile16, full_a, full_b, partial, spread, running, outgoing, incoming,
    gram_buf, square_row, square_col, send_sem, recv_sem,
):
    my_row = lax.axis_index("row")
    my_col = lax.axis_index("col")
    tile_rows, slots, size = entries_ref.shape[:3]
    stored = tile_rows * slots
    order = now_ref.shape[0]
    share = now_ref.shape[1] // size
    col_tiles = n_row * share
    started = []

    def row_peer(k):
        return lax.rem(my_row + k, n_row)

    def col_peer(k):
        return lax.rem(my_col + k, n_col)

    barrier = pltpu.get_barrier_semaphore()
    for k in range(1, n_row):
        pl.semaphore_signal(barrier, inc=1, device_id=(row_peer(k), my_col), device_id_type=MESH)
    for k in range(1, n_col):
        pl.semaphore_signal(barrier, inc=1, device_id=(my_row, col_peer(k)), device_id_type=MESH)

    def send(step, phase, k, source, target, device):
        copy = pltpu.make_async_remote_copy(
            src_ref=source, dst_ref=target,
            send_sem=send_sem.at[step, phase, k], recv_sem=recv_sem.at[step, phase, k],
            device_id=device, device_id_type=MESH,
        )
        copy.start()
        started.append(copy)
        return copy

    def tiles_of(values):
        return [values[:, t * size : (t + 1) * size] for t in range(share)]

    def load(ref):
        return tiles_of(near(ref[...].astype(jnp.float32)))

    current, earlier, earliest = load(now_ref), load(prev_ref), load(prev2_ref)
    gram_old = near(gram_ref[...].astype(jnp.float32))
    square_old = near(square_ref[...].astype(jnp.float32))
    inverse_old = near(inverse_ref[...].astype(jnp.float32))
    inverse_older = near(inverse2_ref[...].astype(jnp.float32))
    identity = identity_of(order)
    fulls = (full_a, full_b)
    for t in range(share):
        full_a[my_row * share + t] = current[t]
    pl.semaphore_wait(barrier, n_row + n_col - 2)

    for step in range(2):
        full = fulls[step]
        mine = full.at[pl.ds(my_row * share, share)]
        gathers = [
            send(step, GATHER, k, mine, mine, (row_peer(k), my_col)) for k in range(1, n_row)
        ]
        if step == 0:
            for i in range(stored):
                tile16[i] = entries_ref[i // slots, i % slots].astype(jnp.float32).astype(jnp.bfloat16)
        middle = near(identity - small_product(inverse_old, gram_old))
        third = -small_product(
            small_product(near(square_old + gram_old), middle), inverse_older
        )
        for copy in gathers:
            copy.wait_recv()

        for r in range(tile_rows):
            total = None
            for s in range(slots):
                picked = full[index_ref[r * slots + s]]
                term = dot_t(digits(picked), tile16[r * slots + s])
                total = term if total is None else total + term
            partial[step, my_col, r] = fold_two(total[:order], total[order:])
        own = partial.at[step, my_col]
        sends = [
            send(step, PARTIAL, k, own, own, (my_row, col_peer(k))) for k in range(1, n_col)
        ]
        for copy in sends:
            copy.wait_recv()
        projected = []
        for r in range(tile_rows):
            total = partial[step, 0, r]
            for c in range(1, n_col):
                total = total + partial[step, c, r]
            projected.append(near(total))

        gram_buf[step, my_row] = gram_tiles(projected)
        own = gram_buf.at[step, my_row]
        grams = [send(step, GRAM, k, own, own, (row_peer(k), my_col)) for k in range(1, n_row)]

        for r in range(tile_rows):
            both = digits(projected[r])
            for s in range(slots):
                spread[r * slots + s] = dot(both, tile16[r * slots + s])
        total = jnp.zeros((2 * order, size), jnp.float32)
        running[0] = total
        for i in range(stored):
            total = total + spread[index_ref[stored + i]]
            running[i + 1] = total
        scatters = []
        for k in list(range(1, n_row)) + [0]:
            peer = row_peer(k)
            for t in range(share):
                tile = peer * share + t
                begin = index_ref[2 * stored + tile]
                end = index_ref[2 * stored + col_tiles + tile]
                summed = running[end] - running[begin]
                outgoing[step, tile] = fold_two(summed[:order], summed[order:])
            if k:
                scatters.append(
                    send(
                        step, SCATTER, k, outgoing.at[step, pl.ds(peer * share, share)],
                        incoming.at[step, my_row], (peer, my_col),
                    )
                )

        for copy in grams:
            copy.wait_recv()
        total = gram_buf[step, 0]
        for r in range(1, n_row):
            total = total + gram_buf[step, r]
        gram_now = near(total)
        inverse_now = inverse_of(gram_now)
        second = -small_product(gram_now, inverse_old)
        parts = []
        for t in range(share):
            one = product_parts(second, earlier[t])
            two = product_parts(third, earliest[t])
            parts.append([a + b for a, b in zip(one, two)])

        for copy in scatters:
            copy.wait_recv()
        applied = []
        for t in range(share):
            total = outgoing[step, my_row * share + t]
            for k in range(1, n_row):
                total = total + incoming[step, row_peer(k), t]
            applied.append(near(total))

        square_row[step, my_row] = gram_tiles(applied)
        own = square_row.at[step, my_row]
        sends = [
            send(step, SQUARE_ROW, k, own, own, (row_peer(k), my_col)) for k in range(1, n_row)
        ]
        for copy in sends:
            copy.wait_recv()
        total = square_row[step, 0]
        for r in range(1, n_row):
            total = total + square_row[step, r]
        square_col[step, my_col] = near(total)
        own = square_col.at[step, my_col]
        sends = [
            send(step, SQUARE_COL, k, own, own, (my_row, col_peer(k))) for k in range(1, n_col)
        ]
        for copy in sends:
            copy.wait_recv()
        total = square_col[step, 0]
        for c in range(1, n_col):
            total = total + square_col[step, c]
        square_now = near(total)

        first = near(identity - small_product(near(square_now + gram_now), inverse_now))
        following = []
        for t in range(share):
            upper, mid, lower = [
                a + b for a, b in zip(product_parts(first, current[t]), parts[t])
            ]
            following.append(
                whole(applied[t] + near(upper) * 15.0 + near(mid) * 256.0 + lower)
            )
        out = (next_ref, later_ref)[step]
        if step == 0:
            for t in range(share):
                full_b[my_row * share + t] = near(following[t])
        for t in range(share):
            out[:, t * size : (t + 1) * size] = following[t] / modulus
        earliest, earlier, current = earlier, current, [near(f) for f in following]
        inverse_older, inverse_old = inverse_old, inverse_now
        gram_old, square_old = gram_now, square_now

    for copy in started:
        copy.wait_send()


def body(
    n_row, n_col, entries, tile_cols, block_now, block_prev, block_prev2,
    gram_prev, square_prev, inverse_prev, inverse_prev2,
):
    tile_rows, slots, size = entries.shape[:3]
    order, width = block_now.shape
    share = width // size
    col_tiles = n_row * share
    stored = tile_rows * slots
    assert tile_rows <= 4 and share <= 4

    cols = tile_cols.reshape(-1)
    places = jnp.arange(stored, dtype=jnp.int32)
    ahead = (cols[None, :] < cols[:, None]) | (
        (cols[None, :] == cols[:, None]) & (places[None, :] < places[:, None])
    )
    rank = jnp.sum(ahead.astype(jnp.int32), axis=1)
    ordered = jnp.sum(jnp.where(rank[None, :] == places[:, None], places[None, :], 0), axis=1)
    tiles = jnp.arange(col_tiles, dtype=jnp.int32)
    begin = jnp.sum((cols[None, :] < tiles[:, None]).astype(jnp.int32), axis=1)
    end = jnp.sum((cols[None, :] <= tiles[:, None]).astype(jnp.int32), axis=1)
    index = jnp.concatenate([cols, ordered, begin, end])

    peers = max(n_row, n_col)
    f32 = jnp.float32
    vmem = pl.BlockSpec(memory_space=pltpu.VMEM)
    return pl.pallas_call(
        functools.partial(kernel, n_row, n_col),
        out_shape=(jax.ShapeDtypeStruct((order, width), f32),) * 2,
        in_specs=[pl.BlockSpec(memory_space=pltpu.SMEM)] + [vmem] * 8,
        out_specs=(vmem, vmem),
        scratch_shapes=[
            pltpu.VMEM((stored, size, size), jnp.bfloat16),
            pltpu.VMEM((col_tiles, order, size), f32),
            pltpu.VMEM((col_tiles, order, size), f32),
            pltpu.VMEM((2, n_col, tile_rows, order, size), f32),
            pltpu.VMEM((stored, 2 * order, size), f32),
            pltpu.VMEM((stored + 1, 2 * order, size), f32),
            pltpu.VMEM((2, col_tiles, order, size), f32),
            pltpu.VMEM((2, n_row, share, order, size), f32),
            pltpu.VMEM((2, n_row, order, order), f32),
            pltpu.VMEM((2, n_row, order, order), f32),
            pltpu.VMEM((2, n_col, order, order), f32),
            pltpu.SemaphoreType.DMA((2, 6, peers)),
            pltpu.SemaphoreType.DMA((2, 6, peers)),
        ],
        compiler_params=pltpu.CompilerParams(collective_id=0, has_side_effects=True),
    )(
        index, entries, block_now, block_prev, block_prev2,
        gram_prev, square_prev, inverse_prev, inverse_prev2,
    )


def solution(mesh):
    placed = (
        P("row", "col", None, None),
        P("row", "col"),
        P(None, ("col", "row")),
        P(None, ("col", "row")),
        P(None, ("col", "row")),
        P(),
        P(),
        P(),
        P(),
    )
    return jax.shard_map(
        functools.partial(body, mesh.shape["row"], mesh.shape["col"]),
        mesh=mesh,
        in_specs=placed,
        out_specs=(P(None, ("col", "row")), P(None, ("col", "row"))),
        check_vma=False,
    )
```

time: 1190 us -> 97.3 us (0.08)
  loops' own time: 641 us -> 0 us
  waiting for transfers between devices: 183 us -> 0 us
  blocking collectives: 146 us -> 0 us
  other arithmetic: 141 us -> 0.98 us
  Pallas kernels: 0 us -> 92.5 us
  local copies, waits for them, and re-layouts: 47.1 us -> 2.9 us
  between operations: 14.5 us -> 0.65 us
    another operation x2 -> x0, loops' own time: 641 us -> none  [inverse_matrix(): augmented = lax.fori_loop(0, matrix_order, eliminate, augmented)]
    reduce_scatter x2 -> x0, waiting for transfers between devices: 125 us -> none  [body(): lax.psum_scatter(partial_term, 'row', scatter_dimension=1, tiled=True)]
    pallas_call x0 -> x1, Pallas kernels: none -> 92.5 us  [body(): pl.pallas_call(functools.partial(kernel, n_row, n_col), out_shape=(jax.Sh...]
    psum x2 -> x0, blocking collectives: 81.1 us -> none  [body(): lax.psum(digit_pair(gram_local(projected_piece, projected_piece)), ('row'...]
    all_gather x2 -> x0, blocking collectives: 64.4 us -> none  [body(): block_full = lax.all_gather(current, 'row', axis=1, tiled=True)]
    psum x2 -> x0, waiting for transfers between devices: 58.7 us -> none  [body(): lax.psum(forward_partial(block_full, tile_values, tile_cols), 'col')]
    another operation x76 -> x0, other arithmetic: 48.5 us -> none  [the longest x64 46.5 us: eliminate(): pivot_row_id = jnp.where(jnp.any(usable), jnp.argmax(usable), column)]
    eq x128 -> x0, other arithmetic: 41.6 us -> none  [the longest x64 41.2 us: eliminate(): return jnp.where((row_numbers == column)[:, None], scaled[None, :], reduced)]
  transfers between devices with their start and end apart: 4 -> 0, of which waited for: 4 -> 0; matrix products, arithmetic and copies ran while one was open for 0% -> 0% of each run, Pallas kernels for 0% -> 0%
where the time goes in v1:
time: 97.3 us; the launch traced here: 97.1 us
  Pallas kernels  92.5 us (95%)
  local copies, waits for them, and re-layouts  2.9 us (3%)
  other arithmetic  0.98 us (1%)
    pallas_call x1, Pallas kernels, body(): pl.pallas_call(functools.partial(kernel, n_row, n_col), out_shape=(jax.Sh...  92.5 us
    unnamed x4, local copies, waits for them, and re-layouts  2.14 us

profile of v1, /device:TPU:0, one launch (start us, length us, event | category | flops | bytes accessed | tf_op | source)
XLA Modules:
  0.0 97.1 jit_solution(10066288208378197675)
XLA Ops:
  0.6 0.8 reshape.10
  1.4 0.2 convert_reduce_fusion.2
  1.6 0.1 select_reduce_fusion
  1.7 0.1 convert_reduce_fusion.1
  1.8 0.6 pad_add_fusion.index_ref
  2.4 92.5 %shard_map.104 = (f32[32,512]{1,0:T(8,128)}, f32[32,512]{1,0:T(8,128)}) custom-call(s32[96]{0:T(128)} %pad_add_fusion.index_ref, s32[4,4,128,128]{3,2,1,0:T(8,128)} %entries_ref.1, s32[32,512]{1,0:T(8,128)} %now_ref.1, s32[32,512]{1,0:T(8,128)} %prev_ref.1, s32[32,512]{1,0:T(8,128)} %prev2_ref.1, s32[32,32]{1,0:T(8,128)} %gram_ref.1, s32[32,32]{1,0:T(8,128)} %square_ref.1, ...), custom_call_target="tpu_custom_call" | custom-call | tf_op jit(solution)/shard_map/pallas_call | solution.py:341
  94.9 0.0 copy-start
  94.9 1.5 %copy.13 = f32[32,512]{1,0:T(8,128)} copy(f32[32,512]{1,0:T(8,128)} %get-tuple-element.6) | data formatting | bytes 131072
  96.4 0.0 copy-done
  96.4 0.6 copy.14
Async XLA Ops:
  94.9 1.5 %copy-start = (f32[32,512]{1,0:T(8,128)S(1)}, f32[32,512]{1,0:T(8,128)}, u32[]{:S(2)}) copy-start(f32[32,512]{1,0:T(8,128)} %get-tuple-element.7) | copy-start | bytes 196612

commit v2 on v1

--- a/solution.py
+++ b/solution.py
@@ -124,8 +124,30 @@
     return mulmod(work[:, order:], power_inverse(diagonal))
 
 
+def pack(values):
+    rows = values.shape[0] // 4
+    return jnp.concatenate([values[g * rows : (g + 1) * rows] for g in range(4)], axis=1)
+
+
+def unpack(values):
+    width = values.shape[1] // 4
+    return jnp.concatenate([values[:, g * width : (g + 1) * width] for g in range(4)], axis=0)
+
+
+def flipped(place, mask, count):
+    assert count & (count - 1) == 0
+    bit = 1
+    moved = place
+    while bit < count:
+        if mask & bit:
+            moved = moved + bit - 2 * bit * lax.rem(place // bit, 2)
+        bit *= 2
+    return moved
+
+
 def kernel(
-    n_row, n_col, index_ref, entries_ref, now_ref, prev_ref, prev2_ref,
+    n_row, n_col, cols_ref, order_ref, begin_ref, end_ref,
+    entries_ref, now_ref, prev_ref, prev2_ref,
     gram_ref, square_ref, inverse_ref, inverse2_ref, next_ref, later_ref,
     tile16, full_a, full_b, partial, spread, running, outgoing, incoming,
     gram_buf, square_row, square_col, send_sem, recv_sem,
@@ -136,20 +158,20 @@
     stored = tile_rows * slots
     order = now_ref.shape[0]
     share = now_ref.shape[1] // size
-    col_tiles = n_row * share
+    half = n_row // 2
     started = []
 
-    def row_peer(k):
-        return lax.rem(my_row + k, n_row)
-
-    def col_peer(k):
-        return lax.rem(my_col + k, n_col)
+    def row_peer(m):
+        return flipped(my_row, m, n_row)
+
+    def col_peer(m):
+        return flipped(my_col, m, n_col)
 
     barrier = pltpu.get_barrier_semaphore()
-    for k in range(1, n_row):
-        pl.semaphore_signal(barrier, inc=1, device_id=(row_peer(k), my_col), device_id_type=MESH)
-    for k in range(1, n_col):
-        pl.semaphore_signal(barrier, inc=1, device_id=(my_row, col_peer(k)), device_id_type=MESH)
+    for m in range(1, n_row):
+        pl.semaphore_signal(barrier, inc=1, device_id=(row_peer(m), my_col), device_id_type=MESH)
+    for m in range(1, n_col):
+        pl.semaphore_signal(barrier, inc=1, device_id=(my_row, col_peer(m)), device_id_type=MESH)
 
     def send(step, phase, k, source, target, device):
         copy = pltpu.make_async_remote_copy(
@@ -167,56 +189,80 @@
     def load(ref):
         return tiles_of(near(ref[...].astype(jnp.float32)))
 
+    def block(full, row):
+        return full.at[pl.ds(row * share, share)]
+
     current, earlier, earliest = load(now_ref), load(prev_ref), load(prev2_ref)
     gram_old = near(gram_ref[...].astype(jnp.float32))
     square_old = near(square_ref[...].astype(jnp.float32))
     inverse_old = near(inverse_ref[...].astype(jnp.float32))
     inverse_older = near(inverse2_ref[...].astype(jnp.float32))
     identity = identity_of(order)
-    fulls = (full_a, full_b)
     for t in range(share):
         full_a[my_row * share + t] = current[t]
     pl.semaphore_wait(barrier, n_row + n_col - 2)
 
-    for step in range(2):
-        full = fulls[step]
-        mine = full.at[pl.ds(my_row * share, share)]
-        gathers = [
-            send(step, GATHER, k, mine, mine, (row_peer(k), my_col)) for k in range(1, n_row)
+    def gather_start(step, full):
+        mine = block(full, my_row)
+        copies = [
+            send(step, GATHER, m, mine, mine, (row_peer(2 * m), my_col)) for m in range(1, half)
         ]
-        if step == 0:
-            for i in range(stored):
-                tile16[i] = entries_ref[i // slots, i % slots].astype(jnp.float32).astype(jnp.bfloat16)
+        copies.append(send(step, GATHER, 0, mine, mine, (row_peer(1), my_col)))
+        return copies
+
+    def gather_finish(step, full, copies):
+        passed = []
+        for m in range(1, half):
+            copies[m - 1].wait_recv()
+            got = block(full, row_peer(2 * m))
+            passed.append(send(step, GATHER, half + m, got, got, (row_peer(1), my_col)))
+        copies[-1].wait_recv()
+        for copy in passed:
+            copy.wait_recv()
+
+    def third_of():
         middle = near(identity - small_product(inverse_old, gram_old))
-        third = -small_product(
+        return -small_product(
             small_product(near(square_old + gram_old), middle), inverse_older
         )
-        for copy in gathers:
-            copy.wait_recv()
-
+
+    gathers = gather_start(0, full_a)
+    for i in range(stored):
+        tile16[i] = entries_ref[i // slots, i % slots].astype(jnp.float32).astype(jnp.bfloat16)
+    third = third_of()
+    gather_finish(0, full_a, gathers)
+
+    def forward(step, full):
+        copies = []
         for r in range(tile_rows):
             total = None
             for s in range(slots):
-                picked = full[index_ref[r * slots + s]]
+                picked = full[cols_ref[r, s]]
                 term = dot_t(digits(picked), tile16[r * slots + s])
                 total = term if total is None else total + term
             partial[step, my_col, r] = fold_two(total[:order], total[order:])
-        own = partial.at[step, my_col]
-        sends = [
-            send(step, PARTIAL, k, own, own, (my_row, col_peer(k))) for k in range(1, n_col)
-        ]
-        for copy in sends:
-            copy.wait_recv()
-        projected = []
-        for r in range(tile_rows):
-            total = partial[step, 0, r]
-            for c in range(1, n_col):
-                total = total + partial[step, c, r]
-            projected.append(near(total))
-
-        gram_buf[step, my_row] = gram_tiles(projected)
+            own = partial.at[step, my_col, r]
+            for m in range(1, n_col):
+                copies.append(
+                    send(step, PARTIAL, r * n_col + m, own, own, (my_row, col_peer(m)))
+                )
+        return copies
+
+    def summed_partial(step, r):
+        total = partial[step, 0, r]
+        for c in range(1, n_col):
+            total = total + partial[step, c, r]
+        return total
+
+    sends = forward(0, full_a)
+    for copy in sends:
+        copy.wait_recv()
+    projected = [near(summed_partial(0, r)) for r in range(tile_rows)]
+
+    for step in range(2):
+        gram_buf[step, my_row] = pack(gram_tiles(projected))
         own = gram_buf.at[step, my_row]
-        grams = [send(step, GRAM, k, own, own, (row_peer(k), my_col)) for k in range(1, n_row)]
+        grams = [send(step, GRAM, m, own, own, (row_peer(m), my_col)) for m in range(1, n_row)]
 
         for r in range(tile_rows):
             both = digits(projected[r])
@@ -225,22 +271,20 @@
         total = jnp.zeros((2 * order, size), jnp.float32)
         running[0] = total
         for i in range(stored):
-            total = total + spread[index_ref[stored + i]]
+            total = total + spread[order_ref[i]]
             running[i + 1] = total
         scatters = []
-        for k in list(range(1, n_row)) + [0]:
-            peer = row_peer(k)
+        for m in range(n_row - 1, -1, -1):
+            peer = row_peer(m)
             for t in range(share):
                 tile = peer * share + t
-                begin = index_ref[2 * stored + tile]
-                end = index_ref[2 * stored + col_tiles + tile]
-                summed = running[end] - running[begin]
+                summed = running[end_ref[tile]] - running[begin_ref[tile]]
                 outgoing[step, tile] = fold_two(summed[:order], summed[order:])
-            if k:
+            if m:
                 scatters.append(
                     send(
-                        step, SCATTER, k, outgoing.at[step, pl.ds(peer * share, share)],
-                        incoming.at[step, my_row], (peer, my_col),
+                        step, SCATTER, m, block(outgoing.at[step], peer),
+                        incoming.at[step, m], (peer, my_col),
                     )
                 )
 
@@ -249,61 +293,73 @@
         total = gram_buf[step, 0]
         for r in range(1, n_row):
             total = total + gram_buf[step, r]
-        gram_now = near(total)
+        gram_now = unpack(near(total))
         inverse_now = inverse_of(gram_now)
         second = -small_product(gram_now, inverse_old)
+        if step:
+            third = third_of()
         parts = []
         for t in range(share):
             one = product_parts(second, earlier[t])
             two = product_parts(third, earliest[t])
-            parts.append([a + b for a, b in zip(one, two)])
+            upper, mid, lower = [a + b for a, b in zip(one, two)]
+            parts.append(near(upper) * 15.0 + near(mid) * 256.0 + lower)
 
         for copy in scatters:
             copy.wait_recv()
         applied = []
         for t in range(share):
             total = outgoing[step, my_row * share + t]
-            for k in range(1, n_row):
-                total = total + incoming[step, row_peer(k), t]
+            for m in range(1, n_row):
+                total = total + incoming[step, m, t]
             applied.append(near(total))
 
-        square_row[step, my_row] = gram_tiles(applied)
+        ready = [near(applied[t] + parts[t]) for t in range(share)]
+        if step == 0:
+            for t in range(share):
+                full_b[my_row * share + t] = ready[t]
+            gathers = gather_start(1, full_b)
+
+        square_row[step, my_row] = pack(gram_tiles(applied))
         own = square_row.at[step, my_row]
-        sends = [
-            send(step, SQUARE_ROW, k, own, own, (row_peer(k), my_col)) for k in range(1, n_row)
+        squares = [
+            send(step, SQUARE_ROW, m, own, own, (row_peer(m), my_col)) for m in range(1, n_row)
         ]
-        for copy in sends:
+        if step == 0:
+            gather_finish(1, full_b, gathers)
+            sends = forward(1, full_b)
+        for copy in squares:
             copy.wait_recv()
         total = square_row[step, 0]
         for r in range(1, n_row):
             total = total + square_row[step, r]
         square_col[step, my_col] = near(total)
         own = square_col.at[step, my_col]
-        sends = [
-            send(step, SQUARE_COL, k, own, own, (my_row, col_peer(k))) for k in range(1, n_col)
+        squares = [
+            send(step, SQUARE_COL, m, own, own, (my_row, col_peer(m))) for m in range(1, n_col)
         ]
-        for copy in sends:
+        for copy in squares:
             copy.wait_recv()
         total = square_col[step, 0]
         for c in range(1, n_col):
             total = total + square_col[step, c]
-        square_now = near(total)
+        square_now = unpack(near(total))
 
         first = near(identity - small_product(near(square_now + gram_now), inverse_now))
+        if step == 0:
+            rest = [fold_three(*product_parts(first, projected[r])) for r in range(tile_rows)]
+            for copy in sends:
+                copy.wait_recv()
+            projected = [near(summed_partial(1, r) + rest[r]) for r in range(tile_rows)]
         following = []
         for t in range(share):
-            upper, mid, lower = [
-                a + b for a, b in zip(product_parts(first, current[t]), parts[t])
-            ]
+            upper, mid, lower = product_parts(first, current[t])
             following.append(
-                whole(applied[t] + near(upper) * 15.0 + near(mid) * 256.0 + lower)
+                whole(ready[t] + near(upper) * 15.0 + near(mid) * 256.0 + lower)
             )
         out = (next_ref, later_ref)[step]
-        if step == 0:
-            for t in range(share):
-                full_b[my_row * share + t] = near(following[t])
         for t in range(share):
-            out[:, t * size : (t + 1) * size] = following[t] / modulus
+            out[:, t * size : (t + 1) * size] = following[t]
         earliest, earlier, current = earlier, current, [near(f) for f in following]
         inverse_older, inverse_old = inverse_old, inverse_now
         gram_old, square_old = gram_now, square_now
@@ -321,27 +377,30 @@
     share = width // size
     col_tiles = n_row * share
     stored = tile_rows * slots
-    assert tile_rows <= 4 and share <= 4
-
-    cols = tile_cols.reshape(-1)
-    places = jnp.arange(stored, dtype=jnp.int32)
-    ahead = (cols[None, :] < cols[:, None]) | (
-        (cols[None, :] == cols[:, None]) & (places[None, :] < places[:, None])
-    )
-    rank = jnp.sum(ahead.astype(jnp.int32), axis=1)
-    ordered = jnp.sum(jnp.where(rank[None, :] == places[:, None], places[None, :], 0), axis=1)
-    tiles = jnp.arange(col_tiles, dtype=jnp.int32)
-    begin = jnp.sum((cols[None, :] < tiles[:, None]).astype(jnp.int32), axis=1)
-    end = jnp.sum((cols[None, :] <= tiles[:, None]).astype(jnp.int32), axis=1)
-    index = jnp.concatenate([cols, ordered, begin, end])
-
-    peers = max(n_row, n_col)
+    assert tile_rows <= 4 and share <= 4 and n_row % 2 == 0
+
+    cols = tile_cols
+    places = jnp.arange(tile_rows, dtype=jnp.int32)[:, None] * slots + jnp.arange(
+        slots, dtype=jnp.int32
+    )
+    mine, other = cols[:, :, None, None], cols[None, None, :, :]
+    ahead = (other < mine) | ((other == mine) & (places[None, None] < places[:, :, None, None]))
+    rank = jnp.sum(ahead.astype(jnp.int32), axis=(2, 3))
+    steps = jnp.arange(stored, dtype=jnp.int32)[:, None, None]
+    ordered = jnp.sum(jnp.where(rank[None] == steps, places[None], 0), axis=(1, 2))
+    tiles = jnp.arange(col_tiles, dtype=jnp.int32)[:, None, None]
+    begin = jnp.sum((cols[None] < tiles).astype(jnp.int32), axis=(1, 2))
+    end = jnp.sum((cols[None] <= tiles).astype(jnp.int32), axis=(1, 2))
+
+    copies = max(n_row + 1, tile_rows * n_col)
     f32 = jnp.float32
+    smem = pl.BlockSpec(memory_space=pltpu.SMEM)
     vmem = pl.BlockSpec(memory_space=pltpu.VMEM)
-    return pl.pallas_call(
+    packed = (order // 4, order * 4)
+    following, later = pl.pallas_call(
         functools.partial(kernel, n_row, n_col),
         out_shape=(jax.ShapeDtypeStruct((order, width), f32),) * 2,
-        in_specs=[pl.BlockSpec(memory_space=pltpu.SMEM)] + [vmem] * 8,
+        in_specs=[smem] * 4 + [vmem] * 8,
         out_specs=(vmem, vmem),
         scratch_shapes=[
             pltpu.VMEM((stored, size, size), jnp.bfloat16),
@@ -352,17 +411,18 @@
             pltpu.VMEM((stored + 1, 2 * order, size), f32),
             pltpu.VMEM((2, col_tiles, order, size), f32),
             pltpu.VMEM((2, n_row, share, order, size), f32),
-            pltpu.VMEM((2, n_row, order, order), f32),
-            pltpu.VMEM((2, n_row, order, order), f32),
-            pltpu.VMEM((2, n_col, order, order), f32),
-            pltpu.SemaphoreType.DMA((2, 6, peers)),
-            pltpu.SemaphoreType.DMA((2, 6, peers)),
+            pltpu.VMEM((2, n_row) + packed, f32),
+            pltpu.VMEM((2, n_row) + packed, f32),
+            pltpu.VMEM((2, n_col) + packed, f32),
+            pltpu.SemaphoreType.DMA((2, 6, copies)),
+            pltpu.SemaphoreType.DMA((2, 6, copies)),
         ],
         compiler_params=pltpu.CompilerParams(collective_id=0, has_side_effects=True),
     )(
-        index, entries, block_now, block_prev, block_prev2,
+        cols, ordered, begin, end, entries, block_now, block_prev, block_prev2,
         gram_prev, square_prev, inverse_prev, inverse_prev2,
     )
+    return following / modulus, later / modulus
 
 
 def solution(mesh):

time: 97.3 us -> 82.8 us (0.85)
  Pallas kernels: 92.5 us -> 77.4 us
  other arithmetic: 0.98 us -> 3.95 us
  local copies, waits for them, and re-layouts: 2.9 us -> 0.61 us
    pallas_call x1, Pallas kernels: 92.5 us -> 77.4 us  [body(): pl.pallas_call(functools.partial(kernel, n_row, n_col), out_shape=(jax.Sh...]
    reduce_sum x3, other arithmetic: 0.39 us -> 2.34 us  [the longest x1 1.28 us: body(): end = jnp.sum((cols[None] <= tiles).astype(jnp.int32), axis=(1, 2))]
    div x0 -> x1, other arithmetic: none -> 1.53 us  [body(): return (following / modulus, later / modulus)]
    unnamed x4 -> x2, local copies, waits for them, and re-layouts: 2.14 us -> 0.61 us
where the time goes in v2:
time: 82.8 us; the launch traced here: 82.6 us
  Pallas kernels  77.4 us (93%)
  other arithmetic  3.95 us (5%)
    pallas_call x1, Pallas kernels, body(): pl.pallas_call(functools.partial(kernel, n_row, n_col), out_shape=(jax.Sh...  77.4 us

profile of v2, /device:TPU:0, one launch (start us, length us, event | category | flops | bytes accessed | tf_op | source)
XLA Modules:
  0.0 82.6 jit_solution(5041195419754908616)
XLA Ops:
  0.6 1.3 %convert_reduce_fusion.1 = (s32[32]{0:T(128)}, s32[32]{0:T(128)}) fusion(s32[4,4]{1,0:T(4,128)} %cols_ref.1), kind=kLoop, calls=%fused_computation.3 | loop fusion | flops 3008 | bytes 320 | tf_op jit(solution)/shard_map/reduce_sum | solution.py:393
  1.9 0.0 copy-start
  1.9 0.1 iota_add_fusion
  2.0 0.6 copy-done
  2.6 0.4 convert_reduce_fusion
  3.1 0.6 select_reduce_fusion.order_ref
  3.7 77.4 %shard_map.104 = (f32[32,512]{1,0:T(8,128)}, f32[32,512]{1,0:T(8,128)}) custom-call(s32[4,4]{1,0:T(4,128)} %cols_ref.1, s32[16]{0:T(128)} %select_reduce_fusion.order_ref, s32[32]{0:T(128)} %get-tuple-element.7.begin_ref, s32[32]{0:T(128)} %get-tuple-element.6.end_ref, s32[4,4,128,128]{3,2,1,0:T(8,128)} %entries_ref.1, s32[32,512]{1,0:T(8,128)} %now_ref.1, ...), custom_call_target="tpu_custom_call" | custom-call | tf_op jit(solution)/shard_map/pallas_call | solution.py:400
  81.1 1.5 %broadcast_multiply_fusion = (f32[32,512]{1,0:T(8,128)}, f32[32,512]{1,0:T(8,128)}) fusion(f32[32,512]{1,0:T(8,128)} %get-tuple-element.5, f32[32,512]{1,0:T(8,128)} %get-tuple-element.4), kind=kLoop, calls=%fused_computation | loop fusion | flops 32768 | bytes 262144 | tf_op jit(solution)/shard_map/div | solution.py:425
  (1 shorter events, 0.0 us)
Async XLA Ops:
  1.9 0.7 copy-start

commit v3 on v2

--- a/solution.py
+++ b/solution.py
@@ -146,11 +146,11 @@
 
 
 def kernel(
-    n_row, n_col, cols_ref, order_ref, begin_ref, end_ref,
+    n_row, n_col, cols_ref,
     entries_ref, now_ref, prev_ref, prev2_ref,
     gram_ref, square_ref, inverse_ref, inverse2_ref, next_ref, later_ref,
-    tile16, full_a, full_b, partial, spread, running, outgoing, incoming,
-    gram_buf, square_row, square_col, send_sem, recv_sem,
+    tile16, full_a0, full_a1, full_b0, full_b1, partial, spread, running, outgoing, incoming,
+    gram_buf, square_row, square_col, order_ref, begin_ref, send_sem, recv_sem,
 ):
     my_row = lax.axis_index("row")
     my_col = lax.axis_index("col")
@@ -159,6 +159,8 @@
     order = now_ref.shape[0]
     share = now_ref.shape[1] // size
     half = n_row // 2
+    part = order // 2
+    fulls = ((full_a0, full_a1), (full_b0, full_b1))
     started = []
 
     def row_peer(m):
@@ -173,10 +175,10 @@
     for m in range(1, n_col):
         pl.semaphore_signal(barrier, inc=1, device_id=(my_row, col_peer(m)), device_id_type=MESH)
 
-    def send(step, phase, k, source, target, device):
+    def send(step, h, phase, k, source, target, device):
         copy = pltpu.make_async_remote_copy(
             src_ref=source, dst_ref=target,
-            send_sem=send_sem.at[step, phase, k], recv_sem=recv_sem.at[step, phase, k],
+            send_sem=send_sem.at[step, h, phase, k], recv_sem=recv_sem.at[step, h, phase, k],
             device_id=device, device_id_type=MESH,
         )
         copy.start()
@@ -198,24 +200,33 @@
     inverse_old = near(inverse_ref[...].astype(jnp.float32))
     inverse_older = near(inverse2_ref[...].astype(jnp.float32))
     identity = identity_of(order)
-    for t in range(share):
-        full_a[my_row * share + t] = current[t]
+
+    def halves(values):
+        return (values[:part], values[part:])
+
+    def fill(step, tiles):
+        for t in range(share):
+            for h, rows in enumerate(halves(tiles[t])):
+                fulls[step][h][my_row * share + t] = rows
+
+    fill(0, current)
     pl.semaphore_wait(barrier, n_row + n_col - 2)
 
-    def gather_start(step, full):
-        mine = block(full, my_row)
+    def gather_start(step, h):
+        mine = block(fulls[step][h], my_row)
         copies = [
-            send(step, GATHER, m, mine, mine, (row_peer(2 * m), my_col)) for m in range(1, half)
+            send(step, h, GATHER, m, mine, mine, (row_peer(2 * m), my_col))
+            for m in range(1, half)
         ]
-        copies.append(send(step, GATHER, 0, mine, mine, (row_peer(1), my_col)))
+        copies.append(send(step, h, GATHER, 0, mine, mine, (row_peer(1), my_col)))
         return copies
 
-    def gather_finish(step, full, copies):
+    def gather_finish(step, h, copies):
         passed = []
         for m in range(1, half):
             copies[m - 1].wait_recv()
-            got = block(full, row_peer(2 * m))
-            passed.append(send(step, GATHER, half + m, got, got, (row_peer(1), my_col)))
+            got = block(fulls[step][h], row_peer(2 * m))
+            passed.append(send(step, h, GATHER, half + m, got, got, (row_peer(1), my_col)))
         copies[-1].wait_recv()
         for copy in passed:
             copy.wait_recv()
@@ -226,67 +237,108 @@
             small_product(near(square_old + gram_old), middle), inverse_older
         )
 
-    gathers = gather_start(0, full_a)
+    gathers = [gather_start(0, h) for h in range(2)]
     for i in range(stored):
         tile16[i] = entries_ref[i // slots, i % slots].astype(jnp.float32).astype(jnp.bfloat16)
+    cols = [cols_ref[i // slots, i % slots] for i in range(stored)]
+
+    def as_int(flag):
+        return jnp.where(flag, 1, 0).astype(jnp.int32)
+
+    ranks = []
+    for i in range(stored):
+        rank = jnp.int32(0)
+        for j in range(stored):
+            if j != i:
+                rank = rank + as_int(cols[j] <= cols[i] if j < i else cols[j] < cols[i])
+        ranks.append(rank)
+    for k in range(stored):
+        place = jnp.int32(0)
+        for i in range(1, stored):
+            place = place + jnp.where(ranks[i] == k, i, 0).astype(jnp.int32)
+        order_ref[k] = place
+
+    def count(tile, carry):
+        below = jnp.int32(0)
+        for i in range(stored):
+            below = below + as_int(cols[i] < tile)
+        begin_ref[tile] = below
+        return carry
+
+    lax.fori_loop(0, n_row * share + 1, count, 0)
     third = third_of()
-    gather_finish(0, full_a, gathers)
-
-    def forward(step, full):
+
+    def forward(step, h):
         copies = []
         for r in range(tile_rows):
             total = None
             for s in range(slots):
-                picked = full[cols_ref[r, s]]
+                picked = fulls[step][h][cols[r * slots + s]]
                 term = dot_t(digits(picked), tile16[r * slots + s])
                 total = term if total is None else total + term
-            partial[step, my_col, r] = fold_two(total[:order], total[order:])
-            own = partial.at[step, my_col, r]
+            partial[step, h, my_col, r] = fold_two(total[:part], total[part:])
+            own = partial.at[step, h, my_col, r]
             for m in range(1, n_col):
                 copies.append(
-                    send(step, PARTIAL, r * n_col + m, own, own, (my_row, col_peer(m)))
+                    send(step, h, PARTIAL, r * n_col + m, own, own, (my_row, col_peer(m)))
                 )
         return copies
 
-    def summed_partial(step, r):
-        total = partial[step, 0, r]
+    def summed_partial(step, h, r):
+        total = partial[step, h, 0, r]
         for c in range(1, n_col):
-            total = total + partial[step, c, r]
+            total = total + partial[step, h, c, r]
         return total
 
-    sends = forward(0, full_a)
-    for copy in sends:
-        copy.wait_recv()
-    projected = [near(summed_partial(0, r)) for r in range(tile_rows)]
+    sends = []
+    for h in range(2):
+        gather_finish(0, h, gathers[h])
+        sends.append(forward(0, h))
+    rest = None
 
     for step in range(2):
-        gram_buf[step, my_row] = pack(gram_tiles(projected))
-        own = gram_buf.at[step, my_row]
-        grams = [send(step, GRAM, m, own, own, (row_peer(m), my_col)) for m in range(1, n_row)]
-
-        for r in range(tile_rows):
-            both = digits(projected[r])
-            for s in range(slots):
-                spread[r * slots + s] = dot(both, tile16[r * slots + s])
-        total = jnp.zeros((2 * order, size), jnp.float32)
-        running[0] = total
-        for i in range(stored):
-            total = total + spread[order_ref[i]]
-            running[i + 1] = total
-        scatters = []
-        for m in range(n_row - 1, -1, -1):
-            peer = row_peer(m)
-            for t in range(share):
-                tile = peer * share + t
-                summed = running[end_ref[tile]] - running[begin_ref[tile]]
-                outgoing[step, tile] = fold_two(summed[:order], summed[order:])
-            if m:
-                scatters.append(
-                    send(
-                        step, SCATTER, m, block(outgoing.at[step], peer),
-                        incoming.at[step, m], (peer, my_col),
+        pieces, scatters = [], []
+        for h in range(2):
+            for copy in sends[h]:
+                copy.wait_recv()
+            piece = []
+            for r in range(tile_rows):
+                total = summed_partial(step, h, r)
+                piece.append(near(total if rest is None else total + halves(rest[r])[h]))
+            pieces.append(piece)
+            if h == 1:
+                projected = [
+                    jnp.concatenate([pieces[0][r], pieces[1][r]], axis=0) for r in range(tile_rows)
+                ]
+                gram_buf[step, my_row] = pack(gram_tiles(projected))
+                own = gram_buf.at[step, my_row]
+                grams = [
+                    send(step, 0, GRAM, m, own, own, (row_peer(m), my_col))
+                    for m in range(1, n_row)
+                ]
+
+            for r in range(tile_rows):
+                both = digits(piece[r])
+                for s in range(slots):
+                    spread[r * slots + s] = dot(both, tile16[r * slots + s])
+            total = jnp.zeros((order, size), jnp.float32)
+            running[0] = total
+            for i in range(stored):
+                total = total + spread[order_ref[i]]
+                running[i + 1] = total
+            for m in range(n_row - 1, -1, -1):
+                peer = row_peer(m)
+                for t in range(share):
+                    tile = peer * share + t
+                    summed = running[begin_ref[tile + 1]] - running[begin_ref[tile]]
+                    outgoing[step, h, tile] = fold_two(summed[:part], summed[part:])
+                if m:
+                    scatters.append(
+                        send(
+                            step, h, SCATTER, m, block(outgoing.at[step, h], peer),
+                            incoming.at[step, h, m], (peer, my_col),
+                        )
                     )
-                )
 
         for copy in grams:
             copy.wait_recv()
@@ -309,25 +361,27 @@
             copy.wait_recv()
         applied = []
         for t in range(share):
-            total = outgoing[step, my_row * share + t]
-            for m in range(1, n_row):
-                total = total + incoming[step, m, t]
-            applied.append(near(total))
+            rows = []
+            for h in range(2):
+                total = outgoing[step, h, my_row * share + t]
+                for m in range(1, n_row):
+                    total = total + incoming[step, h, m, t]
+                rows.append(near(total))
+            applied.append(jnp.concatenate(rows, axis=0))
 
         ready = [near(applied[t] + parts[t]) for t in range(share)]
         if step == 0:
-            for t in range(share):
-                full_b[my_row * share + t] = ready[t]
-            gathers = gather_start(1, full_b)
+            fill(1, ready)
+            gathers = [gather_start(1, h) for h in range(2)]
 
         square_row[step, my_row] = pack(gram_tiles(applied))
         own = square_row.at[step, my_row]
         squares = [
-            send(step, SQUARE_ROW, m, own, own, (row_peer(m), my_col)) for m in range(1, n_row)
+            send(step, 0, SQUARE_ROW, m, own, own, (row_peer(m), my_col)) for m in range(1, n_row)
         ]
         if step == 0:
-            gather_finish(1, full_b, gathers)
-            sends = forward(1, full_b)
+            gather_finish(1, 0, gathers[0])
+            sends = [forward(1, 0)]
         for copy in squares:
             copy.wait_recv()
         total = square_row[step, 0]
@@ -336,8 +390,11 @@
         square_col[step, my_col] = near(total)
         own = square_col.at[step, my_col]
         squares = [
-            send(step, SQUARE_COL, m, own, own, (my_row, col_peer(m))) for m in range(1, n_col)
+            send(step, 0, SQUARE_COL, m, own, own, (my_row, col_peer(m))) for m in range(1, n_col)
         ]
+        if step == 0:
+            gather_finish(1, 1, gathers[1])
+            sends.append(forward(1, 1))
         for copy in squares:
             copy.wait_recv()
         total = square_col[step, 0]
@@ -348,9 +405,6 @@
         first = near(identity - small_product(near(square_now + gram_now), inverse_now))
         if step == 0:
             rest = [fold_three(*product_parts(first, projected[r])) for r in range(tile_rows)]
-            for copy in sends:
-                copy.wait_recv()
-            projected = [near(summed_partial(1, r) + rest[r]) for r in range(tile_rows)]
         following = []
         for t in range(share):
             upper, mid, lower = product_parts(first, current[t])
@@ -379,47 +433,39 @@
     stored = tile_rows * slots
     assert tile_rows <= 4 and share <= 4 and n_row % 2 == 0
 
-    cols = tile_cols
-    places = jnp.arange(tile_rows, dtype=jnp.int32)[:, None] * slots + jnp.arange(
-        slots, dtype=jnp.int32
-    )
-    mine, other = cols[:, :, None, None], cols[None, None, :, :]
-    ahead = (other < mine) | ((other == mine) & (places[None, None] < places[:, :, None, None]))
-    rank = jnp.sum(ahead.astype(jnp.int32), axis=(2, 3))
-    steps = jnp.arange(stored, dtype=jnp.int32)[:, None, None]
-    ordered = jnp.sum(jnp.where(rank[None] == steps, places[None], 0), axis=(1, 2))
-    tiles = jnp.arange(col_tiles, dtype=jnp.int32)[:, None, None]
-    begin = jnp.sum((cols[None] < tiles).astype(jnp.int32), axis=(1, 2))
-    end = jnp.sum((cols[None] <= tiles).astype(jnp.int32), axis=(1, 2))
-
     copies = max(n_row + 1, tile_rows * n_col)
     f32 = jnp.float32
     smem = pl.BlockSpec(memory_space=pltpu.SMEM)
     vmem = pl.BlockSpec(memory_space=pltpu.VMEM)
     packed = (order // 4, order * 4)
+    part = order // 2
     following, later = pl.pallas_call(
         functools.partial(kernel, n_row, n_col),
         out_shape=(jax.ShapeDtypeStruct((order, width), f32),) * 2,
-        in_specs=[smem] * 4 + [vmem] * 8,
+        in_specs=[smem] + [vmem] * 8,
         out_specs=(vmem, vmem),
         scratch_shapes=[
             pltpu.VMEM((stored, size, size), jnp.bfloat16),
-            pltpu.VMEM((col_tiles, order, size), f32),
-            pltpu.VMEM((col_tiles, order, size), f32),
-            pltpu.VMEM((2, n_col, tile_rows, order, size), f32),
-            pltpu.VMEM((stored, 2 * order, size), f32),
-            pltpu.VMEM((stored + 1, 2 * order, size), f32),
-            pltpu.VMEM((2, col_tiles, order, size), f32),
-            pltpu.VMEM((2, n_row, share, order, size), f32),
+            pltpu.VMEM((col_tiles, part, size), f32),
+            pltpu.VMEM((col_tiles, part, size), f32),
+            pltpu.VMEM((col_tiles, part, size), f32),
+            pltpu.VMEM((col_tiles, part, size), f32),
+            pltpu.VMEM((2, 2, n_col, tile_rows, part, size), f32),
+            pltpu.VMEM((stored, order, size), f32),
+            pltpu.VMEM((stored + 1, order, size), f32),
+            pltpu.VMEM((2, 2, col_tiles, part, size), f32),
+            pltpu.VMEM((2, 2, n_row, share, part, size), f32),
             pltpu.VMEM((2, n_row) + packed, f32),
             pltpu.VMEM((2, n_row) + packed, f32),
             pltpu.VMEM((2, n_col) + packed, f32),
-            pltpu.SemaphoreType.DMA((2, 6, copies)),
-            pltpu.SemaphoreType.DMA((2, 6, copies)),
+            pltpu.SMEM((stored,), jnp.int32),
+            pltpu.SMEM((col_tiles + 1,), jnp.int32),
+            pltpu.SemaphoreType.DMA((2, 2, 6, copies)),
+            pltpu.SemaphoreType.DMA((2, 2, 6, copies)),
         ],
         compiler_params=pltpu.CompilerParams(collective_id=0, has_side_effects=True),
     )(
-        cols, ordered, begin, end, entries, block_now, block_prev, block_prev2,
+        tile_cols, entries, block_now, block_prev, block_prev2,
         gram_prev, square_prev, inverse_prev, inverse_prev2,
     )
     return following / modulus, later / modulus

time: 82.8 us -> 84 us (1.014)
  Pallas kernels: 77.4 us -> 81.6 us
  other arithmetic: 3.95 us -> 1.53 us
    pallas_call x1, Pallas kernels: 77.4 us -> 81.6 us  [body(): pl.pallas_call(functools.partial(kernel, n_row, n_col), out_shape=(jax.Sh...]
    reduce_sum x3 -> x0, other arithmetic: 2.34 us -> none  [the longest x1 1.28 us: body(): end = jnp.sum((cols[None] <= tiles).astype(jnp.int32), axis=(1, 2))]
where the time goes in v3:
time: 84 us; the launch traced here: 83.8 us
  Pallas kernels  81.6 us (97%)
  other arithmetic  1.53 us (2%)
    pallas_call x1, Pallas kernels, body(): pl.pallas_call(functools.partial(kernel, n_row, n_col), out_shape=(jax.Sh...  81.6 us

profile of v3, /device:TPU:0, one launch (start us, length us, event | category | flops | bytes accessed | tf_op | source)
XLA Modules:
  0.0 83.8 jit_solution(18345050458559366041)
XLA Ops:
  0.6 81.6 %shard_map.104 = (f32[32,512]{1,0:T(8,128)}, f32[32,512]{1,0:T(8,128)}) custom-call(s32[4,4]{1,0:T(4,128)} %cols_ref.1, s32[4,4,128,128]{3,2,1,0:T(8,128)} %entries_ref.1, s32[32,512]{1,0:T(8,128)} %now_ref.1, s32[32,512]{1,0:T(8,128)} %prev_ref.1, s32[32,512]{1,0:T(8,128)} %prev2_ref.1, s32[32,32]{1,0:T(8,128)} %gram_ref.1, s32[32,32]{1,0:T(8,128)} %square_ref.1, ...), custom_call_target="tpu_custom_call" | custom-call | tf_op jit(solution)/shard_map/pallas_call | solution.py:442
  82.2 1.5 %broadcast_multiply_fusion = (f32[32,512]{1,0:T(8,128)}, f32[32,512]{1,0:T(8,128)}) fusion(f32[32,512]{1,0:T(8,128)} %get-tuple-element.5, f32[32,512]{1,0:T(8,128)} %get-tuple-element.4), kind=kLoop, calls=%fused_computation | loop fusion | flops 32768 | bytes 262144 | tf_op jit(solution)/shard_map/div | solution.py:471

commit v4 on v2

--- a/solution.py
+++ b/solution.py
@@ -146,11 +146,11 @@
 
 
 def kernel(
-    n_row, n_col, cols_ref, order_ref, begin_ref, end_ref,
+    n_row, n_col, cols_ref,
     entries_ref, now_ref, prev_ref, prev2_ref,
     gram_ref, square_ref, inverse_ref, inverse2_ref, next_ref, later_ref,
     tile16, full_a, full_b, partial, spread, running, outgoing, incoming,
-    gram_buf, square_row, square_col, send_sem, recv_sem,
+    gram_buf, square_row, square_col, order_ref, begin_ref, send_sem, recv_sem,
 ):
     my_row = lax.axis_index("row")
     my_col = lax.axis_index("col")
@@ -229,6 +229,32 @@
     gathers = gather_start(0, full_a)
     for i in range(stored):
         tile16[i] = entries_ref[i // slots, i % slots].astype(jnp.float32).astype(jnp.bfloat16)
+    cols = [cols_ref[i // slots, i % slots] for i in range(stored)]
+
+    def as_int(flag):
+        return jnp.where(flag, 1, 0).astype(jnp.int32)
+
+    ranks = []
+    for i in range(stored):
+        rank = jnp.int32(0)
+        for j in range(stored):
+            if j != i:
+                rank = rank + as_int(cols[j] <= cols[i] if j < i else cols[j] < cols[i])
+        ranks.append(rank)
+    for k in range(stored):
+        place = jnp.int32(0)
+        for i in range(1, stored):
+            place = place + jnp.where(ranks[i] == k, i, 0).astype(jnp.int32)
+        order_ref[k] = place
+
+    def count(tile, carry):
+        below = jnp.int32(0)
+        for i in range(stored):
+            below = below + as_int(cols[i] < tile)
+        begin_ref[tile] = below
+        return carry
+
+    lax.fori_loop(0, n_row * share + 1, count, 0)
     third = third_of()
     gather_finish(0, full_a, gathers)
 
@@ -237,7 +263,7 @@
         for r in range(tile_rows):
             total = None
             for s in range(slots):
-                picked = full[cols_ref[r, s]]
+                picked = full[cols[r * slots + s]]
                 term = dot_t(digits(picked), tile16[r * slots + s])
                 total = term if total is None else total + term
             partial[step, my_col, r] = fold_two(total[:order], total[order:])
@@ -278,7 +304,7 @@
             peer = row_peer(m)
             for t in range(share):
                 tile = peer * share + t
-                summed = running[end_ref[tile]] - running[begin_ref[tile]]
+                summed = running[begin_ref[tile + 1]] - running[begin_ref[tile]]
                 outgoing[step, tile] = fold_two(summed[:order], summed[order:])
             if m:
                 scatters.append(
@@ -379,19 +405,6 @@
     stored = tile_rows * slots
     assert tile_rows <= 4 and share <= 4 and n_row % 2 == 0
 
-    cols = tile_cols
-    places = jnp.arange(tile_rows, dtype=jnp.int32)[:, None] * slots + jnp.arange(
-        slots, dtype=jnp.int32
-    )
-    mine, other = cols[:, :, None, None], cols[None, None, :, :]
-    ahead = (other < mine) | ((other == mine) & (places[None, None] < places[:, :, None, None]))
-    rank = jnp.sum(ahead.astype(jnp.int32), axis=(2, 3))
-    steps = jnp.arange(stored, dtype=jnp.int32)[:, None, None]
-    ordered = jnp.sum(jnp.where(rank[None] == steps, places[None], 0), axis=(1, 2))
-    tiles = jnp.arange(col_tiles, dtype=jnp.int32)[:, None, None]
-    begin = jnp.sum((cols[None] < tiles).astype(jnp.int32), axis=(1, 2))
-    end = jnp.sum((cols[None] <= tiles).astype(jnp.int32), axis=(1, 2))
-
     copies = max(n_row + 1, tile_rows * n_col)
     f32 = jnp.float32
     smem = pl.BlockSpec(memory_space=pltpu.SMEM)
@@ -400,7 +413,7 @@
     following, later = pl.pallas_call(
         functools.partial(kernel, n_row, n_col),
         out_shape=(jax.ShapeDtypeStruct((order, width), f32),) * 2,
-        in_specs=[smem] * 4 + [vmem] * 8,
+        in_specs=[smem] + [vmem] * 8,
         out_specs=(vmem, vmem),
         scratch_shapes=[
             pltpu.VMEM((stored, size, size), jnp.bfloat16),
@@ -414,12 +427,14 @@
             pltpu.VMEM((2, n_row) + packed, f32),
             pltpu.VMEM((2, n_row) + packed, f32),
             pltpu.VMEM((2, n_col) + packed, f32),
+            pltpu.SMEM((stored,), jnp.int32),
+            pltpu.SMEM((col_tiles + 1,), jnp.int32),
             pltpu.SemaphoreType.DMA((2, 6, copies)),
             pltpu.SemaphoreType.DMA((2, 6, copies)),
         ],
         compiler_params=pltpu.CompilerParams(collective_id=0, has_side_effects=True),
     )(
-        cols, ordered, begin, end, entries, block_now, block_prev, block_prev2,
+        tile_cols, entries, block_now, block_prev, block_prev2,
         gram_prev, square_prev, inverse_prev, inverse_prev2,
     )
     return following / modulus, later / modulus

time: 82.8 us -> 79.7 us (0.963)
  other arithmetic: 3.95 us -> 1.53 us
    reduce_sum x3 -> x0, other arithmetic: 2.34 us -> none  [the longest x1 1.28 us: body(): end = jnp.sum((cols[None] <= tiles).astype(jnp.int32), axis=(1, 2))]
where the time goes in v4:
time: 79.7 us; the launch traced here: 79.6 us
  Pallas kernels  77.4 us (97%)
  other arithmetic  1.53 us (2%)
    pallas_call x1, Pallas kernels, body(): pl.pallas_call(functools.partial(kernel, n_row, n_col), out_shape=(jax.Sh...  77.4 us

profile of v4, /device:TPU:0, one launch (start us, length us, event | category | flops | bytes accessed | tf_op | source)
XLA Modules:
  0.0 79.6 jit_solution(1533998767844762768)
XLA Ops:
  0.6 77.4 %shard_map.104 = (f32[32,512]{1,0:T(8,128)}, f32[32,512]{1,0:T(8,128)}) custom-call(s32[4,4]{1,0:T(4,128)} %cols_ref.1, s32[4,4,128,128]{3,2,1,0:T(8,128)} %entries_ref.1, s32[32,512]{1,0:T(8,128)} %now_ref.1, s32[32,512]{1,0:T(8,128)} %prev_ref.1, s32[32,512]{1,0:T(8,128)} %prev2_ref.1, s32[32,32]{1,0:T(8,128)} %gram_ref.1, s32[32,32]{1,0:T(8,128)} %square_ref.1, ...), custom_call_target="tpu_custom_call" | custom-call | tf_op jit(solution)/shard_map/pallas_call | solution.py:413
  78.0 1.5 %broadcast_multiply_fusion = (f32[32,512]{1,0:T(8,128)}, f32[32,512]{1,0:T(8,128)}) fusion(f32[32,512]{1,0:T(8,128)} %get-tuple-element.5, f32[32,512]{1,0:T(8,128)} %get-tuple-element.4), kind=kLoop, calls=%fused_computation | loop fusion | flops 32768 | bytes 262144 | tf_op jit(solution)/shard_map/div | solution.py:440

commit v5 on v4

--- a/solution.py
+++ b/solution.py
@@ -299,20 +299,37 @@
         for i in range(stored):
             total = total + spread[order_ref[i]]
             running[i + 1] = total
-        scatters = []
-        for m in range(n_row - 1, -1, -1):
-            peer = row_peer(m)
+        def finish_block(peer):
             for t in range(share):
                 tile = peer * share + t
                 summed = running[begin_ref[tile + 1]] - running[begin_ref[tile]]
                 outgoing[step, tile] = fold_two(summed[:order], summed[order:])
-            if m:
-                scatters.append(
-                    send(
-                        step, SCATTER, m, block(outgoing.at[step], peer),
-                        incoming.at[step, m], (peer, my_col),
-                    )
+
+        across = {}
+        for m in range(half - 1, -1, -1):
+            peer = row_peer(2 * m + 1)
+            finish_block(peer)
+            across[m] = send(
+                step, SCATTER, m, block(outgoing.at[step], peer),
+                incoming.at[step, m], (row_peer(1), my_col),
+            )
+        for m in range(half - 1, -1, -1):
+            finish_block(row_peer(2 * m))
+        scatters = []
+        for m in range(half - 1, 0, -1):
+            across[m].wait_recv()
+            peer = row_peer(2 * m)
+            for t in range(share):
+                outgoing[step, peer * share + t] = (
+                    outgoing[step, peer * share + t] + incoming[step, m, t]
                 )
+            scatters.append(
+                send(
+                    step, SCATTER, half + m, block(outgoing.at[step], peer),
+                    incoming.at[step, half + m], (peer, my_col),
+                )
+            )
+        scatters.append(across[0])
 
         for copy in grams:
             copy.wait_recv()
@@ -336,7 +353,7 @@
         applied = []
         for t in range(share):
             total = outgoing[step, my_row * share + t]
-            for m in range(1, n_row):
+            for m in [0] + list(range(half + 1, n_row)):
                 total = total + incoming[step, m, t]
             applied.append(near(total))
 

time: 79.7 us -> 74.8 us (0.939)
  Pallas kernels: 77.4 us -> 72.5 us
    pallas_call x1, Pallas kernels: 77.4 us -> 72.5 us  [body(): pl.pallas_call(functools.partial(kernel, n_row, n_col), out_shape=(jax.Sh...]
where the time goes in v5:
time: 74.8 us; the launch traced here: 74.6 us
  Pallas kernels  72.5 us (97%)
  other arithmetic  1.53 us (2%)
    pallas_call x1, Pallas kernels, body(): pl.pallas_call(functools.partial(kernel, n_row, n_col), out_shape=(jax.Sh...  72.5 us
    div x1, other arithmetic, body(): return (following / modulus, later / modulus)  1.53 us

profile of v5, /device:TPU:0, one launch (start us, length us, event | category | flops | bytes accessed | tf_op | source)
XLA Modules:
  0.0 74.6 jit_solution(16819790293528847349)
XLA Ops:
  0.6 72.5 %shard_map.104 = (f32[32,512]{1,0:T(8,128)}, f32[32,512]{1,0:T(8,128)}) custom-call(s32[4,4]{1,0:T(4,128)} %cols_ref.1, s32[4,4,128,128]{3,2,1,0:T(8,128)} %entries_ref.1, s32[32,512]{1,0:T(8,128)} %now_ref.1, s32[32,512]{1,0:T(8,128)} %prev_ref.1, s32[32,512]{1,0:T(8,128)} %prev2_ref.1, s32[32,32]{1,0:T(8,128)} %gram_ref.1, s32[32,32]{1,0:T(8,128)} %square_ref.1, ...), custom_call_target="tpu_custom_call" | custom-call | tf_op jit(solution)/shard_map/pallas_call | solution.py:430
  73.1 1.5 %broadcast_multiply_fusion = (f32[32,512]{1,0:T(8,128)}, f32[32,512]{1,0:T(8,128)}) fusion(f32[32,512]{1,0:T(8,128)} %get-tuple-element.5, f32[32,512]{1,0:T(8,128)} %get-tuple-element.4), kind=kLoop, calls=%fused_computation | loop fusion | flops 32768 | bytes 262144 | tf_op jit(solution)/shard_map/div | solution.py:457
